TPU v7x, 32 devices: a whole 2x2x4 slice. The times are simulated.
32 devices in a mesh: dp: 8 (over z, y), tensor: 4 (over x, core).
Axes of the slice: x: 2, y: 2, z: 4, core: 2. Of those that a mesh axis runs over, the one named last changes fastest.
Arguments:
- tokens: bfloat16 [12288, 768], P('dp', 'tensor'), may hold values from -6 to 6
- cotangent: bfloat16 [12288, 768], P('dp', 'tensor'), may hold values from -6 to 6
- seq_start: int32 [12288], P('dp'), may hold values from 0 to 384, as said below
- row_place: int32 [8, 1536], P('dp'), may hold values from 0 to 1535, each once within a row
- qkv_weight: bfloat16 [3, 768, 768], P(None, None, 'tensor'), may hold values from -0.21875 to 0.21875
- qv_bias: bfloat16 [2, 768], P(None, 'tensor'), may hold values from -1.5 to 1.5
- out_weight: bfloat16 [768, 768], P('tensor'), may hold values from -0.875 to 0.875
- out_bias: bfloat16 [768], replicated, may hold values from -1.5 to 1.5
- first_gain: bfloat16 [768], replicated, may hold values from 0.5 to 1.5
- first_shift: bfloat16 [768], replicated, may hold values from -1.5 to 1.5
- up_weight: bfloat16 [2, 768, 3072], P(None, None, 'tensor'), may hold values from -0.21875 to 0.21875
- up_bias: bfloat16 [2, 3072], P(None, 'tensor'), may hold values from -1.5 to 1.5
- down_weight: bfloat16 [3072, 768], P('tensor'), may hold values from -0.15625 to 0.15625
- down_bias: bfloat16 [768], replicated, may hold values from -1.5 to 1.5
- second_gain: bfloat16 [768], replicated, may hold values from 0.5 to 1.5
- second_shift: bfloat16 [768], replicated, may hold values from -1.5 to 1.5
Outputs:
- layer_out: bfloat16 [12288, 768], P('dp', 'tensor')
- input_grad: bfloat16 [12288, 768], P('dp', 'tensor')
- qkv_grad: float32 [3, 768, 768], P(None, 'dp', 'tensor')
- qv_bias_grad: float32 [2, 768], P(None, 'tensor')
- out_grad: float32 [768, 768], P('tensor', 'dp')
- out_bias_grad: float32 [768], P('dp')
- first_gain_grad: float32 [768], P('dp')
- first_shift_grad: float32 [768], P('dp')
- up_grad: float32 [2, 768, 3072], P(None, 'dp', 'tensor')
- up_bias_grad: float32 [2, 3072], P(None, 'tensor')
- down_grad: float32 [3072, 768], P('tensor', 'dp')
- down_bias_grad: float32 [768], P('dp')
- second_gain_grad: float32 [768], P('dp')
- second_shift_grad: float32 [768], P('dp')
Inputs may be any that keep to these rules, and one draw needn't show every extreme that they name: seq_start of a token is the offset, within its aligned block of 512 packed rows, of the first token of its sequence; sequences are 128, 256 or 512 tokens long, begin at multiples of 128 and never cross a block. Each row of row_place is a permutation of 0 to 1535.
All inputs are finite; a program needn't handle non-finite values.
Results may differ from a plain program's by a relative error of at most 0.02.
The roundings to bfloat16 on the way count: a program that leaves them out, or rounds other values in their place, can miss the bound.
Values may be sent and summed in bfloat16 or wider, within the bound.
A program may use at most 128 MiB of HBM per device.

v0:
```python
import jax
import jax.numpy as jnp
from jax import lax
from jax.sharding import PartitionSpec as P

HEADS = 12
HEAD_DIM = 64
BLOCK = 512


def layer_norm(values, scale_row, shift_row):
    center = values - jnp.mean(values, axis=-1, keepdims=True)
    spread = jnp.mean(center * center, axis=-1, keepdims=True)
    return center * lax.rsqrt(spread + 1e-05) * scale_row + shift_row


def gated_unit(gate_part, value_part):
    return jax.nn.gelu(gate_part, approximate=False) * value_part


def alibi_terms(part_index, local_heads, block_rows):
    heads_idx = (part_index * local_heads + jnp.arange(local_heads)).astype(jnp.float32)
    slopes = 2.0 ** (-8.0 * (heads_idx + 1.0) / HEADS)
    position = jnp.arange(block_rows).astype(jnp.float32)
    distance = jnp.abs(position[:, None] - position[None, :])
    return -slopes[:, None, None] * distance[None]


def block_scores(queries, key_rows, alibi_bias, same_seq, score_scale):
    raw_scores = jnp.einsum(
        "bqhe,bkhe->bhqk", queries, key_rows, preferred_element_type=jnp.float32
    )
    scored = raw_scores * score_scale + alibi_bias[None]
    return jnp.where(same_seq[:, None], scored, -1e30)


def softmax_rows(scored):
    row_max = jnp.max(scored, axis=-1, keepdims=True)
    exponent = jnp.exp(scored - row_max)
    denominator = jnp.sum(exponent, axis=-1, keepdims=True)
    return (exponent / denominator, row_max + jnp.log(denominator))


def on_device(
    tokens,
    cotangent,
    seq_start,
    row_place,
    qkv_weight,
    qv_bias,
    out_weight,
    out_bias,
    first_gain,
    first_shift,
    up_weight,
    up_bias,
    down_weight,
    down_bias,
    second_gain,
    second_shift,
):
    arr_tokens, arr_cot = (
        lax.all_to_all(tokens, "dp", split_axis=0, concat_axis=0, tiled=True),
        lax.all_to_all(cotangent, "dp", split_axis=0, concat_axis=0, tiled=True),
    )
    wide_tokens, wide_cot = (
        lax.all_gather(arr_tokens, "tensor", axis=1, tiled=True),
        lax.all_gather(arr_cot, "tensor", axis=1, tiled=True),
    )
    slot_index = row_place[0]
    packed_in = jnp.zeros_like(wide_tokens).at[slot_index].set(wide_tokens)
    packed_cot = jnp.zeros_like(wide_cot).at[slot_index].set(wide_cot)
    row_count = packed_in.shape[0]
    columns = packed_in.shape[1]
    local_heads = qkv_weight.shape[2] // HEAD_DIM
    block_rows = BLOCK
    blocks = row_count // block_rows
    part_index = lax.axis_index("tensor")
    col_count = columns // lax.axis_size("tensor")
    score_scale = HEAD_DIM ** (-0.5)
    alibi_bias = alibi_terms(part_index, local_heads, block_rows)
    block_starts = seq_start.reshape(blocks, block_rows)
    same_seq = block_starts[:, :, None] == block_starts[:, None, :]
    bias_rows = jnp.stack([qv_bias[0], jnp.zeros_like(qv_bias[0]), qv_bias[1]]).astype(jnp.float32)
    projected = jnp.einsum("td,kde->kte", packed_in, qkv_weight, preferred_element_type=jnp.float32)
    qkv_rows = (projected + bias_rows[:, None, :]).astype(jnp.bfloat16)
    split_heads = qkv_rows.reshape(3, blocks, block_rows, local_heads, HEAD_DIM)
    queries = split_heads[0]
    key_rows = split_heads[1]
    value_rows = split_heads[2]
    attn_probs, log_total = softmax_rows(
        block_scores(queries, key_rows, alibi_bias, same_seq, score_scale)
    )
    context = jnp.einsum(
        "bhqk,bkhe->bqhe",
        attn_probs.astype(jnp.bfloat16),
        value_rows,
        preferred_element_type=jnp.float32,
    )
    context = context.reshape(row_count, local_heads * HEAD_DIM).astype(jnp.bfloat16)
    attn_part = jnp.dot(context, out_weight, preferred_element_type=jnp.float32)
    attended = lax.psum(attn_part, "tensor")
    hidden = packed_in.astype(jnp.float32) + (attended + out_bias.astype(jnp.float32))
    normed, first_pull = jax.vjp(
        layer_norm, hidden, first_gain.astype(jnp.float32), first_shift.astype(jnp.float32)
    )
    normed_low = normed.astype(jnp.bfloat16)
    lifted = jnp.einsum("td,kdf->ktf", normed_low, up_weight, preferred_element_type=jnp.float32)
    lifted = lifted + up_bias.astype(jnp.float32)[:, None, :]
    gated_val, gate_pull = jax.vjp(gated_unit, lifted[0], lifted[1])
    gated_low = gated_val.astype(jnp.bfloat16)
    ffn_part = jnp.dot(gated_low, down_weight, preferred_element_type=jnp.float32)
    ffn_out = lax.psum(ffn_part.astype(jnp.bfloat16), "tensor").astype(jnp.float32)
    mixed_rows = normed + (ffn_out + down_bias.astype(jnp.float32))
    result, second_pull = jax.vjp(
        layer_norm, mixed_rows, second_gain.astype(jnp.float32), second_shift.astype(jnp.float32)
    )
    grad_scale = (row_count * lax.axis_size("dp")) ** (-0.5)
    d_mixed, d_second_gain, d_second_shift = second_pull(packed_cot.astype(jnp.float32))
    d_mixed_low = d_mixed.astype(jnp.bfloat16)
    g_down = jnp.einsum("tf,td->fd", gated_low, d_mixed_low, preferred_element_type=jnp.float32)
    g_down_bias = jnp.sum(d_mixed, axis=0)
    d_gated = jnp.einsum("td,fd->tf", d_mixed_low, down_weight, preferred_element_type=jnp.float32)
    d_gate, d_value = gate_pull(d_gated)
    d_lifted = jnp.stack([d_gate, d_value]).astype(jnp.bfloat16)
    g_up = jnp.einsum("td,ktf->kdf", normed_low, d_lifted, preferred_element_type=jnp.float32)
    g_up_bias = jnp.sum(d_lifted, axis=1, dtype=jnp.float32)
    d_normed_part = jnp.einsum(
        "ktf,kdf->td", d_lifted, up_weight, preferred_element_type=jnp.float32
    )
    d_normed = d_mixed + lax.psum(d_normed_part.astype(jnp.bfloat16), "tensor").astype(jnp.float32)
    d_hidden, d_first_gain, d_first_shift = first_pull(d_normed)
    d_hidden_low = d_hidden.astype(jnp.bfloat16)
    g_out = jnp.einsum("te,td->ed", context, d_hidden_low, preferred_element_type=jnp.float32)
    g_out_bias = jnp.sum(d_hidden, axis=0)
    d_context = jnp.einsum(
        "td,ed->te", d_hidden_low, out_weight, preferred_element_type=jnp.float32
    )
    d_context = d_context.astype(jnp.bfloat16).reshape(blocks, block_rows, local_heads, HEAD_DIM)
    probs_back = jnp.exp(
        block_scores(queries, key_rows, alibi_bias, same_seq, score_scale) - log_total
    )
    d_probs = jnp.einsum(
        "bqhe,bkhe->bhqk", d_context, value_rows, preferred_element_type=jnp.float32
    )
    g_values = jnp.einsum(
        "bhqk,bqhe->bkhe",
        probs_back.astype(jnp.bfloat16),
        d_context,
        preferred_element_type=jnp.float32,
    )
    center_term = jnp.sum(probs_back * d_probs, axis=-1, keepdims=True)
    d_scores = (probs_back * (d_probs - center_term)).astype(jnp.bfloat16)
    g_queries = (
        jnp.einsum("bhqk,bkhe->bqhe", d_scores, key_rows, preferred_element_type=jnp.float32)
        * score_scale
    )
    g_keys = (
        jnp.einsum("bhqk,bqhe->bkhe", d_scores, queries, preferred_element_type=jnp.float32)
        * score_scale
    )
    d_qkv = jnp.stack([g_queries, g_keys, g_values]).reshape(3, row_count, local_heads * HEAD_DIM)
    d_qkv = d_qkv.astype(jnp.bfloat16)
    g_qkv = jnp.einsum("td,kte->kde", packed_in, d_qkv, preferred_element_type=jnp.float32)
    g_qv_bias = jnp.sum(jnp.stack([d_qkv[0], d_qkv[2]]), axis=1, dtype=jnp.float32)
    d_input_part = jnp.einsum("kte,kde->td", d_qkv, qkv_weight, preferred_element_type=jnp.float32)
    hidden_cols = lax.dynamic_slice_in_dim(d_hidden, part_index * col_count, col_count, 1)
    grad_cols = hidden_cols + lax.psum_scatter(
        d_input_part.astype(jnp.bfloat16), "tensor", scatter_dimension=1, tiled=True
    ).astype(jnp.float32)
    summed = (
        lax.psum_scatter(g_qkv * grad_scale, "dp", scatter_dimension=1, tiled=True),
        lax.psum_scatter(g_out * grad_scale, "dp", scatter_dimension=1, tiled=True),
        lax.psum_scatter(g_out_bias * grad_scale, "dp", scatter_dimension=0, tiled=True),
        lax.psum_scatter(d_first_gain * grad_scale, "dp", scatter_dimension=0, tiled=True),
        lax.psum_scatter(d_first_shift * grad_scale, "dp", scatter_dimension=0, tiled=True),
        lax.psum_scatter(g_up * grad_scale, "dp", scatter_dimension=1, tiled=True),
        lax.psum_scatter(g_down * grad_scale, "dp", scatter_dimension=1, tiled=True),
        lax.psum_scatter(g_down_bias * grad_scale, "dp", scatter_dimension=0, tiled=True),
        lax.psum_scatter(d_second_gain * grad_scale, "dp", scatter_dimension=0, tiled=True),
        lax.psum_scatter(d_second_shift * grad_scale, "dp", scatter_dimension=0, tiled=True),
    )
    qkv_grad, out_grad, out_bias_grad, first_gain_grad, first_shift_grad = (
        summed[0],
        summed[1],
        summed[2],
        summed[3],
        summed[4],
    )
    up_grad, down_grad, down_bias_grad, second_gain_grad, second_shift_grad = (
        summed[5],
        summed[6],
        summed[7],
        summed[8],
        summed[9],
    )
    qv_bias_grad, up_bias_grad = lax.psum((g_qv_bias * grad_scale, g_up_bias * grad_scale), "dp")
    layer_cols = lax.dynamic_slice_in_dim(result, part_index * col_count, col_count, 1)
    layer_back = layer_cols[slot_index].astype(jnp.bfloat16)
    grad_back = grad_cols[slot_index].astype(jnp.bfloat16)
    layer_out, input_grad = (
        lax.all_to_all(layer_back, "dp", split_axis=0, concat_axis=0, tiled=True),
        lax.all_to_all(grad_back, "dp", split_axis=0, concat_axis=0, tiled=True),
    )
    return (
        layer_out,
        input_grad,
        qkv_grad,
        qv_bias_grad,
        out_grad,
        out_bias_grad,
        first_gain_grad,
        first_shift_grad,
        up_grad,
        up_bias_grad,
        down_grad,
        down_bias_grad,
        second_gain_grad,
        second_shift_grad,
    )


def solution(mesh):
    return jax.shard_map(
        on_device,
        mesh=mesh,
        in_specs=(
            P("dp", "tensor"),
            P("dp", "tensor"),
            P("dp"),
            P("dp", None),
            P(None, None, "tensor"),
            P(None, "tensor"),
            P("tensor", None),
            P(),
            P(),
            P(),
            P(None, None, "tensor"),
            P(None, "tensor"),
            P("tensor", None),
            P(),
            P(),
            P(),
        ),
        out_specs=(
            P("dp", "tensor"),
            P("dp", "tensor"),
            P(None, "dp", "tensor"),
            P(None, "tensor"),
            P("tensor", "dp"),
            P("dp"),
            P("dp"),
            P("dp"),
            P(None, "dp", "tensor"),
            P(None, "tensor"),
            P("tensor", "dp"),
            P("dp"),
            P("dp"),
            P("dp"),
        ),
        check_vma=False,
    )
```

profile of v0, /device:TPU:0, one launch (start us, length us, event | category | flops | bytes accessed | tf_op | source)
XLA Modules:
  0.0 849.5 jit_solution(2268085062084630268)
XLA Ops:
  9.3 27.3 %all_to_all.42 = bf16[8,192,192]{1,2,0:T(8,128)(2,1)S(1)} all-to-all(bf16[8,192,192]{1,2,0:T(8,128)(2,1)S(1)} %copy.124), channel_id=1, replica_groups=mesh['dp'=8,'tensor'=4] {'dp'}, dimensions={0} | all-to-all | bytes 1179648 | tf_op jit(solution)/shard_map/all_to_all | solution.py:63
  42.5 19.2 %all-gather.3.cloned.1.call-done = bf16[1536,768]{0,1:T(8,128)(2,1)} async-done(((bf16[1536,192]{0,1:T(8,128)(2,1)}), bf16[1536,768]{0,1:T(8,128)(2,1)}) %all-gather.3.cloned.1.call-update) | async-done | bytes 2359312 | tf_op jit(solution)/shard_map/all_gather | solution.py:67
  61.7 4.3 copy.126
  66.0 10.1 %scatter_custom_fusion = bf16[1536,768]{1,0:T(8,128)(2,1)} fusion(s32[1536]{0:T(1024)S(1)} %fusion.70, bf16[1536,768]{1,0:T(8,128)(2,1)} %copy.126, bf16[]{:T(256)} %constant.46.clone.1), kind=kCustom, calls=%fused_computation.108 | custom fusion | bytes 2359808 | tf_op jit(solution)/shard_map/scatter | solution.py:71
  76.1 3.2 fusion.86
  84.3 5.3 fusion.85
  95.9 2.9 fusion.87
  103.5 5.5 all-to-all-start.2
  109.2 20.5 %all-to-all-done.2 = bf16[8,192,192]{1,2,0:T(8,128)(2,1)} async-done(((bf16[8,192,192]{1,2,0:T(8,128)(2,1)}), bf16[8,192,192]{1,2,0:T(8,128)(2,1)}, u32[]{:S(2)}, u32[]{:S(2)}) %all-to-all-start.2) | async-done | bytes 589856 | tf_op jit(solution)/shard_map/all_to_all | solution.py:64
  134.9 58.2 %all-reduce.13.cloned.1.call-done = f32[1536,768]{1,0:T(8,128)} async-done(((f32[1536,768]{1,0:T(8,128)}), f32[1536,768]{1,0:T(8,128)}) %all-reduce.13.cloned.1.call-update) | async-done | bytes 4718608 | tf_op jit(solution)/shard_map/psum | solution.py:102
  193.1 3.8 fusion.82
  197.6 4.3 add_bitcast_fusion
  201.9 11.5 %multiply_convert_fusion.2 = (bf16[1536,768]{1,0:T(8,128)(2,1)S(1)}, f32[1536,768]{1,0:T(8,128)}) fusion(f32[2,1536,768]{2,1,0:T(8,128)S(1)} %add_bitcast_fusion), kind=kLoop, calls=%fused_computation.51 | loop fusion | flops 77856768 | bytes 16515072 | tf_op jit(solution)/shard_map/convert_element_type | solution.py:111
  214.9 3.5 convolution_convert_fusion
  219.5 4.3 copy.135
  223.7 9.8 %scatter_custom_fusion.1 = bf16[1536,768]{1,0:T(8,128)(2,1)} fusion(s32[1536]{0:T(1024)} %copy-done.29, bf16[1536,768]{1,0:T(8,128)(2,1)} %copy.135, bf16[]{:T(256)} %constant.46.clone.1), kind=kCustom, calls=%fused_computation.106 | custom fusion | bytes 2359808 | tf_op jit(solution)/shard_map/scatter | solution.py:72
  233.6 43.8 %all-reduce.15.cloned.1.call-done = bf16[1536,768]{1,0:T(8,128)(2,1)} async-done(((bf16[1536,768]{1,0:T(8,128)(2,1)}), bf16[1536,768]{1,0:T(8,128)(2,1)}) %all-reduce.15.cloned.1.call-update) | async-done | bytes 2359312 | tf_op jit(solution)/shard_map/psum | solution.py:113
  277.4 4.2 fusion.80
  281.7 2.7 fusion.4
  284.4 4.7 fusion.79
  289.2 7.1 fusion.36
  297.7 7.0 bitcast_convert_fusion.1
  305.8 54.8 %all-reduce.17.cloned.1.call-done = bf16[1536,768]{1,0:T(8,128)(2,1)} async-done(((bf16[1536,768]{1,0:T(8,128)(2,1)}), bf16[1536,768]{1,0:T(8,128)(2,1)}) %all-reduce.17.cloned.1.call-update) | async-done | bytes 2359312 | tf_op jit(solution)/shard_map/psum | solution.py:131
  360.6 6.5 multiply_reduce_fusion.1
  367.1 5.0 fusion.78
  376.9 5.3 fusion.48
  382.2 7.2 multiply_reduce_fusion
  389.4 11.2 %multiply_convert_fusion = bf16[3,3,512,512]{2,3,1,0:T(8,128)(2,1)} fusion(f32[3,3,512,512]{2,3,1,0:T(8,128)} %get-tuple-element.127, f32[3,3,512,512]{2,3,1,0:T(8,128)} %copy-done.2, f32[3,3,512]{2,1,0:T(4,128)S(1)} %get-tuple-element.126, f32[3,3,512]{2,1,0:T(4,128)S(1)} %copy-done.23), kind=kLoop, calls=%fused_computation.5 | loop fusion | flops 9437184 | bytes 23629824 | tf_op jit(solution)/shard_map/convert_element_type | solution.py:153
  400.6 4.0 fusion.51
  407.9 2.7 copy.140
  417.0 4.6 fusion.31
  421.7 3.1 convolution_multiply_fusion.3
  426.1 4.5 multiply_bitcast_fusion.1
  430.6 4.2 copy.162
  434.9 4.8 reshape.283
  439.8 9.6 %multiply_bitcast_fusion = f32[2,768,768]{1,2,0:T(8,128)} fusion(bf16[1,1536,768]{2,1,0:T(8,128)(2,1)} %get-tuple-element.114, bf16[1,1536,768]{2,1,0:T(8,128)(2,1)S(1)} %copy-done.19, f32[1536,768]{1,0:T(8,128)} %copy-done.3, f32[768]{0:T(1024)S(1)} %copy-done.34, f32[768]{0:T(1024)S(1)} %copy-done.28, f32[1536]{0:T(1024)S(1)} %fusion.68, ...), kind=kOutput, calls=%fused_computation.43 | convolution fusion | flops 3633315840 | bytes 14174208 | tf_op jit(solution)/shard_map/td,ktf->kdf/dot_general | solution.py:126
  449.4 8.3 copy.150
  459.3 6.0 convolution_multiply_fusion
  467.7 5.4 gather_fusion
  473.0 5.3 all-to-all-start.1
  479.6 3.1 convert_reduce_fusion
  482.7 17.3 %all-to-all-done.1 = bf16[8,192,192]{2,1,0:T(8,128)(2,1)S(1)} async-done(((bf16[8,192,192]{2,1,0:T(8,128)(2,1)}), bf16[8,192,192]{2,1,0:T(8,128)(2,1)S(1)}, u32[]{:S(2)}, u32[]{:S(2)}) %all-to-all-start.1) | async-done | bytes 589856 | tf_op jit(solution)/shard_map/all_to_all | solution.py:202
  504.7 5.4 gather_fusion.1
  510.0 3.7 all-to-all-start.3
  515.3 44.6 %all-reduce.7 = (f32[2,192]{1,0:T(2,128)}, f32[768]{0:T(1024)S(1)}, f32[768]{0:T(1024)S(1)}, f32[768]{0:T(1024)S(1)}, f32[2,768]{1,0:T(2,128)}, /*index=5*/f32[7...) all-reduce(f32[2,192]{1,0:T(2,128)S(1)} %broadcast_multiply_fusion.10, ...), channel_id=1, replica_groups=mesh['dp'=8,'tensor'=4] {'dp'}, use_global_device_ids=true, to_apply=%region_19.20 | all-reduce | flops 6528 | bytes 52224 | tf_op jit(solution)/shard_map/psum | solution.py:197
  565.0 32.5 %reduce-scatter.15.cloned.1.call-done = f32[96,576]{1,0:T(8,128)} async-done(((f32[768,576]{1,0:T(8,128)}), f32[96,576]{1,0:T(8,128)}) %reduce-scatter.15.cloned.1.call-update) | async-done | bytes 221200
  599.4 170.4 %all-reduce.19.cloned.1.call-done = f32[2,768,768]{2,0,1:T(2,128)} async-done(((f32[2,768,768]{2,0,1:T(2,128)}), f32[2,768,768]{2,0,1:T(2,128)}) %all-reduce.19.cloned.1.call-update) | async-done | bytes 4718608
  772.8 69.6 %reduce-scatter.11.cloned.1.call-done = f32[768,96]{0,1:T(8,128)} async-done(((f32[768,768]{0,1:T(8,128)}), f32[768,96]{0,1:T(8,128)}) %reduce-scatter.11.cloned.1.call-update) | async-done | bytes 294928 | tf_op jit(solution)/shard_map/reduce_scatter | solution.py:178
  (224 shorter events, 71.1 us)
Async XLA Ops:
  7.2 190.4 %copy-start = (bf16[2,768,768]{2,1,0:T(8,128)(2,1)S(1)}, bf16[2,768,768]{2,1,0:T(8,128)(2,1)}, u32[]{:S(2)}) copy-start(bf16[2,768,768]{2,1,0:T(8,128)(2,1)} %param.26) | copy-start | bytes 7077892
  7.2 31.4 %copy-start.39 = (s32[1536]{0:T(1024)S(1)}, s32[1536]{0:T(1024)}, u32[]{:S(2)}) copy-start(s32[1536]{0:T(1024)} %param.18) | copy-start | bytes 18436
  7.2 31.5 %copy-start.40 = (s32[1,1536]{1,0:T(1,128)S(1)}, s32[1,1536]{1,0:T(1,128)}, u32[]{:S(2)}) copy-start(s32[1,1536]{1,0:T(1,128)} %param.19) | copy-start | bytes 18436
  7.2 31.5 %copy-start.43 = (bf16[2,192]{1,0:T(2,128)(2,1)S(1)}, bf16[2,192]{1,0:T(2,128)(2,1)}, u32[]{:S(2)}) copy-start(bf16[2,192]{1,0:T(2,128)(2,1)} %param.21) | copy-start | bytes 2308
  7.2 54.5 %all-gather.3.cloned.1.call-start = ((), (), s32[]{:S(2)}) async-start(), calls=%async_computation.8 | async-start | bytes 2949120 | tf_op jit(solution)/shard_map/all_gather | solution.py:67
  38.5 154.5 %all-reduce.13.cloned.1.call-start = ((), (), s32[]{:S(2)}) async-start(), calls=%async_computation.9 | async-start | bytes 9437184 | tf_op jit(solution)/shard_map/psum | solution.py:102
  38.8 27.3 %copy-start.29 = (s32[1536]{0:T(1024)}, s32[1536]{0:T(1024)S(1)}, u32[]{:S(2)}) copy-start(s32[1536]{0:T(1024)S(1)} %fusion.70) | copy-start | bytes 18436
  40.4 35.7 %copy-start.51 = (bf16[3,768,192]{1,2,0:T(8,128)(2,1)S(1)}, bf16[3,768,192]{1,2,0:T(8,128)(2,1)}, u32[]{:S(2)}) copy-start(bf16[3,768,192]{1,2,0:T(8,128)(2,1)} %param.20) | copy-start | bytes 2654212
  84.3 5.3 copy-start.11
  98.9 10.2 %copy-start.45 = (bf16[768]{0:T(1024)(128)(2,1)S(1)}, bf16[768]{0:T(1024)(128)(2,1)}, u32[]{:S(2)}) copy-start(bf16[768]{0:T(1024)(128)(2,1)} %param.24) | copy-start | bytes 4612
  98.9 10.2 %copy-start.46 = (bf16[768]{0:T(1024)(128)(2,1)S(1)}, bf16[768]{0:T(1024)(128)(2,1)}, u32[]{:S(2)}) copy-start(bf16[768]{0:T(1024)(128)(2,1)} %param.25) | copy-start | bytes 4612
  98.9 10.3 %copy-start.47 = (bf16[768]{0:T(1024)(128)(2,1)S(1)}, bf16[768]{0:T(1024)(128)(2,1)}, u32[]{:S(2)}) copy-start(bf16[768]{0:T(1024)(128)(2,1)} %param.23) | copy-start | bytes 4612
  98.9 10.3 %copy-start.44 = (bf16[2,768]{1,0:T(2,128)(2,1)S(1)}, bf16[2,768]{1,0:T(2,128)(2,1)}, u32[]{:S(2)}) copy-start(bf16[2,768]{1,0:T(2,128)(2,1)} %param.27) | copy-start | bytes 9220
  103.5 26.2 %all-to-all-start.2 = ((bf16[8,192,192]{1,2,0:T(8,128)(2,1)}), bf16[8,192,192]{1,2,0:T(8,128)(2,1)}, u32[]{:S(2)}, u32[]{:S(2)}) async-start(bf16[8,192,192]{1,2,0:T(8,128)(2,1)} %copy.133), calls=%async_computation.2 | async-start | bytes 1572864 | tf_op jit(solution)/shard_map/all_to_all | solution.py:64
  109.1 110.4 %all-gather.5.cloned.1.call-start = ((), (), s32[]{:S(2)}) async-start(), calls=%async_computation.11 | async-start | bytes 2949120 | tf_op jit(solution)/shard_map/all_gather | solution.py:68
  109.1 258.0 %copy-start.27 = (f32[768]{0:T(1024)}, f32[768]{0:T(1024)S(1)}, u32[]{:S(2)}) copy-start(f32[768]{0:T(1024)S(1)} %convert_element_type.142) | copy-start | bytes 9220
  109.2 168.2 %copy-start.33 = (f32[768]{0:T(1024)}, f32[768]{0:T(1024)S(1)}, u32[]{:S(2)}) copy-start(f32[768]{0:T(1024)S(1)} %convert_element_type.143) | copy-start | bytes 9220
  134.7 142.7 %all-reduce.15.cloned.1.call-start = ((), (), s32[]{:S(2)}) async-start(), calls=%async_computation.10 | async-start | bytes 4718592 | tf_op jit(solution)/shard_map/psum | solution.py:113
  201.9 11.5 %copy-start.8 = (f32[2,1536,768]{2,1,0:T(8,128)}, f32[2,1536,768]{2,1,0:T(8,128)S(1)}, u32[]{:S(2)}) copy-start(f32[2,1536,768]{2,1,0:T(8,128)S(1)} %add_bitcast_fusion) | copy-start | bytes 28311556
  201.9 13.0 %copy-start.50 = (bf16[768,768]{1,0:T(8,128)(2,1)S(1)}, bf16[768,768]{1,0:T(8,128)(2,1)}, u32[]{:S(2)}) copy-start(bf16[768,768]{1,0:T(8,128)(2,1)} %param.28) | copy-start | bytes 3538948
  218.4 142.2 %all-reduce.17.cloned.1.call-start = ((), (), s32[]{:S(2)}) async-start(), calls=%async_computation.12 | async-start | bytes 4718592 | tf_op jit(solution)/shard_map/psum | solution.py:131
  281.6 7.5 slice-start
  281.7 7.5 slice-start.3
  289.1 7.2 copy-start.6
  289.1 78.0 %copy-start.25 = (f32[1536]{0:T(1024)}, f32[1536]{0:T(1024)S(1)}, u32[]{:S(2)}) copy-start(f32[1536]{0:T(1024)S(1)} %negate_multiply_fusion.2) | copy-start | bytes 18436
  304.7 196.4 %reduce-scatter.13.cloned.1.call-start = ((), (), s32[]{:S(2)}) async-start(), calls=%async_computation.14 | async-start | bytes 2949120
  360.6 6.5 copy-start.10
  376.9 5.3 copy-start.17
  389.4 11.2 %copy-start.12 = (bf16[3,512,3,64]{1,0,3,2:T(4,128)(2,1)S(1)}, bf16[3,512,3,64]{1,0,3,2:T(4,128)(2,1)}, u32[]{:S(2)}) copy-start(bf16[3,512,3,64]{1,0,3,2:T(4,128)(2,1)} %copy-done.11) | copy-start | bytes 1769476
  407.9 13.8 %copy-start.13 = (bf16[1,1536,192]{1,2,0:T(8,128)(2,1)}, bf16[1,1536,192]{1,2,0:T(8,128)(2,1)S(1)}, u32[]{:S(2)}) copy-start(bf16[1,1536,192]{1,2,0:T(8,128)(2,1)S(1)} %stack.36) | copy-start | bytes 1769476
  412.4 9.3 %copy-start.14 = (bf16[1,1536,192]{1,2,0:T(8,128)(2,1)}, bf16[1,1536,192]{1,2,0:T(8,128)(2,1)S(1)}, u32[]{:S(2)}) copy-start(bf16[1,1536,192]{1,2,0:T(8,128)(2,1)S(1)} %stack.34) | copy-start | bytes 1769476
  421.7 141.7 %reduce-scatter.17.cloned.1.call-start = ((), (), s32[]{:S(2)}) async-start(), calls=%async_computation.16 | async-start | bytes 884736
  426.0 171.4 %reduce-scatter.15.cloned.1.call-start = ((), (), s32[]{:S(2)}) async-start(), calls=%async_computation.15 | async-start | bytes 2211840
  439.7 330.1 %all-reduce.19.cloned.1.call-start = ((), (), s32[]{:S(2)}) async-start(), calls=%async_computation.17 | async-start | bytes 9437184
  457.7 7.6 copy-start.42
  457.7 7.7 copy-start.49
  457.7 7.8 copy-start.30
  457.7 384.7 %reduce-scatter.11.cloned.1.call-start = ((), (), s32[]{:S(2)}) async-start(), calls=%async_computation.13 | async-start | bytes 2654208 | tf_op jit(solution)/shard_map/reduce_scatter | solution.py:178
  467.7 10.7 %copy-start.52 = (u32[32]{0:T(128)S(1)}, u32[32]{0:T(128)}, u32[]{:S(2)}) copy-start(u32[32]{0:T(128)} %constant.120) | copy-start | bytes 388
  467.7 11.9 %copy-start.35 = (f32[768]{0:T(1024)S(1)}, f32[768]{0:T(1024)}, u32[]{:S(2)}) copy-start(f32[768]{0:T(1024)} %get-tuple-element.115) | copy-start | bytes 9220
  473.0 27.0 %all-to-all-start.1 = ((bf16[8,192,192]{2,1,0:T(8,128)(2,1)}), bf16[8,192,192]{2,1,0:T(8,128)(2,1)S(1)}, u32[]{:S(2)}, u32[]{:S(2)}) async-start(bf16[8,192,192]{2,1,0:T(8,128)(2,1)} %bitcast.11), calls=%async_computation.1 | async-start | bytes 1572864 | tf_op jit(solution)/shard_map/all_to_all | solution.py:202
  504.6 10.6 %copy-start.31 = (f32[768]{0:T(1024)S(1)}, f32[768]{0:T(1024)}, u32[]{:S(2)}) copy-start(f32[768]{0:T(1024)} %get-tuple-element.101) | copy-start | bytes 9220
  504.6 10.6 %copy-start.32 = (f32[768]{0:T(1024)S(1)}, f32[768]{0:T(1024)}, u32[]{:S(2)}) copy-start(f32[768]{0:T(1024)} %get-tuple-element.90) | copy-start | bytes 9220
  504.6 10.6 %copy-start.38 = (f32[768]{0:T(1024)S(1)}, f32[768]{0:T(1024)}, u32[]{:S(2)}) copy-start(f32[768]{0:T(1024)} %get-tuple-element.84) | copy-start | bytes 9220
  504.6 10.6 %copy-start.36 = (f32[768]{0:T(1024)S(1)}, f32[768]{0:T(1024)}, u32[]{:S(2)}) copy-start(f32[768]{0:T(1024)} %get-tuple-element.86) | copy-start | bytes 9220
  504.7 10.6 %copy-start.37 = (f32[768]{0:T(1024)S(1)}, f32[768]{0:T(1024)}, u32[]{:S(2)}) copy-start(f32[768]{0:T(1024)} %get-tuple-element.87) | copy-start | bytes 9220
  504.7 337.7 %copy-start.1 = (bf16[2,768,768]{2,1,0:T(8,128)(2,1)S(1)}, bf16[2,768,768]{2,1,0:T(8,128)(2,1)}, u32[]{:S(2)}) copy-start(bf16[2,768,768]{2,1,0:T(8,128)(2,1)} %param.26) | copy-start | bytes 7077892
  510.0 261.7 %all-to-all-start.3 = ((bf16[8,192,192]{2,1,0:T(8,128)(2,1)}), bf16[8,192,192]{2,1,0:T(8,128)(2,1)S(1)}, u32[]{:S(2)}, u32[]{:S(2)}) async-start(bf16[8,192,192]{2,1,0:T(8,128)(2,1)} %bitcast.200), calls=%async_computation.3 | async-start | bytes 1572864 | tf_op jit(solution)/shard_map/all_to_all | solution.py:203
  (23 other events, 81.2 us)
Sparse Core Ops, SparseCore 0:
  38.7 23.0 all-gather.2
  99.0 94.0 all-reduce.12
  195.2 24.1 all-gather.4
  221.7 55.6 all-reduce.14
  304.8 55.7 all-reduce.16
  421.8 32.8 reduce-scatter.12
  458.0 66.9 reduce-scatter.16
  528.5 68.9 reduce-scatter.14
  601.1 168.6 all-reduce.18
  773.7 68.6 reduce-scatter.10
where the time goes:
time: 856 us; the launch traced here: 849 us
  waiting for transfers between devices  487 us (57%)
  local copies, waits for them, and re-layouts  110 us (13%)
  matrix products  82.2 us (10%)
  blocking collectives  71.8 us (8%)
  other arithmetic  66.4 us (8%)
  between operations  16.1 us (2%)
  starting transfers between devices  15.7 us (2%)
    unnamed x14, waiting for transfers between devices  203 us
    reduce_scatter x1, waiting for transfers between devices, on_device(): lax.psum_scatter(g_down * grad_scale, 'dp', scatter_dimension=1, tiled=True)  69.6 us
    psum x1, waiting for transfers between devices, on_device(): attended = lax.psum(attn_part, 'tensor')  58.2 us
    psum x1, waiting for transfers between devices, on_device(): lax.psum(d_normed_part.astype(jnp.bfloat16), 'tensor').astype(jnp.float32)  54.8 us
    psum x1, blocking collectives, on_device(): lax.psum((g_qv_bias * grad_scale, g_up_bias * grad_scale), 'dp')  44.6 us
    psum x1, waiting for transfers between devices, on_device(): lax.psum(ffn_part.astype(jnp.bfloat16), 'tensor').astype(jnp.float32)  43.8 us
    unnamed x135, local copies, waits for them, and re-layouts  31.6 us
    all_to_all x1, blocking collectives, on_device(): lax.all_to_all(tokens, 'dp', split_axis=0, concat_axis=0, tiled=True)  27.3 us
  transfers between devices with their start and end apart: 13, of which 10 were waited for; matrix products, arithmetic and copies ran while one was open for 14% of the time, Pallas kernels for 0%

commit v1 on v0

--- a/solution.py
+++ b/solution.py
@@ -128,7 +128,9 @@
     d_normed_part = jnp.einsum(
         "ktf,kdf->td", d_lifted, up_weight, preferred_element_type=jnp.float32
     )
-    d_normed = d_mixed + lax.psum(d_normed_part.astype(jnp.bfloat16), "tensor").astype(jnp.float32)
+    d_normed = d_mixed + jnp.sum(
+        lax.all_gather(d_normed_part.astype(jnp.bfloat16), axis_name="tensor"), axis=0
+    ).astype(jnp.float32)
     d_hidden, d_first_gain, d_first_shift = first_pull(d_normed)
     d_hidden_low = d_hidden.astype(jnp.bfloat16)
     g_out = jnp.einsum("te,td->ed", context, d_hidden_low, preferred_element_type=jnp.float32)

time: 856 us -> 889 us (1.039)
  waiting for transfers between devices: 487 us -> 523 us
  blocking collectives: 71.8 us -> 62.3 us
    all_gather x0 -> x1, waiting for transfers between devices: none -> 64.4 us  [on_device(): lax.all_gather(d_normed_part.astype(jnp.bfloat16), axis_name='tensor')]
    psum x1 -> x0, waiting for transfers between devices: 54.8 us -> none  [on_device(): lax.psum(d_normed_part.astype(jnp.bfloat16), 'tensor').astype(jnp.float32)]
    all_to_all x1, waiting for transfers between devices: 17.3 us -> 37.9 us  [on_device(): lax.all_to_all(layer_back, 'dp', split_axis=0, concat_axis=0, tiled=True)]
    psum x1, blocking collectives: 44.6 us -> 35.1 us  [on_device(): lax.psum((g_qv_bias * grad_scale, g_up_bias * grad_scale), 'dp')]
  transfers between devices with their start and end apart: 13 -> 13, of which waited for: 10 -> 11; matrix products, arithmetic and copies ran while one was open for 14% -> 14% of each run, Pallas kernels for 0% -> 0%
where the time goes in v1:
time: 889 us; the launch traced here: 882 us
  waiting for transfers between devices  523 us (59%)
  local copies, waits for them, and re-layouts  110 us (12%)
  matrix products  84.1 us (9%)
  other arithmetic  71.8 us (8%)
  blocking collectives  62.3 us (7%)
  between operations  16.1 us (2%)
  starting transfers between devices  15.3 us (2%)
    unnamed x14, waiting for transfers between devices  208 us
    reduce_scatter x1, waiting for transfers between devices, on_device(): lax.psum_scatter(g_down * grad_scale, 'dp', scatter_dimension=1, tiled=True)  69.5 us
    all_gather x1, waiting for transfers between devices, on_device(): lax.all_gather(d_normed_part.astype(jnp.bfloat16), axis_name='tensor')  64.4 us
    psum x1, waiting for transfers between devices, on_device(): attended = lax.psum(attn_part, 'tensor')  58.2 us
    psum x1, waiting for transfers between devices, on_device(): lax.psum(ffn_part.astype(jnp.bfloat16), 'tensor').astype(jnp.float32)  43.8 us
    all_to_all x1, waiting for transfers between devices, on_device(): lax.all_to_all(layer_back, 'dp', split_axis=0, concat_axis=0, tiled=True)  37.9 us
    psum x1, blocking collectives, on_device(): lax.psum((g_qv_bias * grad_scale, g_up_bias * grad_scale), 'dp')  35.1 us
    unnamed x135, local copies, waits for them, and re-layouts  31.3 us
  transfers between devices with their start and end apart: 13, of which 11 were waited for; matrix products, arithmetic and copies ran while one was open for 14% of the time, Pallas kernels for 0%

profile of v1, /device:TPU:0, one launch (start us, length us, event | category | flops | bytes accessed | tf_op | source)
XLA Modules:
  0.0 882.3 jit_solution(8722522916748703831)
XLA Ops:
  9.3 27.3 %all_to_all.42 = bf16[8,192,192]{1,2,0:T(8,128)(2,1)S(1)} all-to-all(bf16[8,192,192]{1,2,0:T(8,128)(2,1)S(1)} %copy.124), channel_id=1, replica_groups=mesh['dp'=8,'tensor'=4] {'dp'}, dimensions={0} | all-to-all | bytes 1179648 | tf_op jit(solution)/shard_map/all_to_all | solution.py:63
  42.5 19.2 %all-gather.5.cloned.1.call-done = bf16[1536,768]{0,1:T(8,128)(2,1)} async-done(((bf16[1536,192]{0,1:T(8,128)(2,1)}), bf16[1536,768]{0,1:T(8,128)(2,1)}) %all-gather.5.cloned.1.call-update) | async-done | bytes 2359312 | tf_op jit(solution)/shard_map/all_gather | solution.py:67
  61.7 4.3 copy.126
  66.0 10.1 %scatter_custom_fusion = bf16[1536,768]{1,0:T(8,128)(2,1)} fusion(s32[1536]{0:T(1024)S(1)} %fusion.70, bf16[1536,768]{1,0:T(8,128)(2,1)} %copy.126, bf16[]{:T(256)} %constant.46.clone.1), kind=kCustom, calls=%fused_computation.108 | custom fusion | bytes 2359808 | tf_op jit(solution)/shard_map/scatter | solution.py:71
  76.1 3.2 fusion.86
  84.3 5.3 fusion.85
  95.9 2.9 fusion.87
  103.5 5.5 all-to-all-start.2
  109.2 20.5 %all-to-all-done.2 = bf16[8,192,192]{1,2,0:T(8,128)(2,1)} async-done(((bf16[8,192,192]{1,2,0:T(8,128)(2,1)}), bf16[8,192,192]{1,2,0:T(8,128)(2,1)}, u32[]{:S(2)}, u32[]{:S(2)}) %all-to-all-start.2) | async-done | bytes 589856 | tf_op jit(solution)/shard_map/all_to_all | solution.py:64
  134.9 58.2 %all-reduce.12.cloned.1.call-done = f32[1536,768]{1,0:T(8,128)} async-done(((f32[1536,768]{1,0:T(8,128)}), f32[1536,768]{1,0:T(8,128)}) %all-reduce.12.cloned.1.call-update) | async-done | bytes 4718608 | tf_op jit(solution)/shard_map/psum | solution.py:102
  193.0 3.8 fusion.82
  197.5 4.3 add_bitcast_fusion
  201.8 11.5 %multiply_convert_fusion.2 = (bf16[1536,768]{1,0:T(8,128)(2,1)S(1)}, f32[1536,768]{1,0:T(8,128)}) fusion(f32[2,1536,768]{2,1,0:T(8,128)S(1)} %add_bitcast_fusion), kind=kLoop, calls=%fused_computation.51 | loop fusion | flops 77856768 | bytes 16515072 | tf_op jit(solution)/shard_map/convert_element_type | solution.py:111
  214.8 3.4 convolution_convert_fusion
  219.4 4.3 copy.135
  223.7 9.8 %scatter_custom_fusion.1 = bf16[1536,768]{1,0:T(8,128)(2,1)} fusion(s32[1536]{0:T(1024)S(1)} %fusion.70, bf16[1536,768]{1,0:T(8,128)(2,1)} %copy.135, bf16[]{:T(256)} %constant.46.clone.1), kind=kCustom, calls=%fused_computation.106 | custom fusion | bytes 2359808 | tf_op jit(solution)/shard_map/scatter | solution.py:72
  233.5 43.8 %all-reduce.14.cloned.1.call-done = bf16[1536,768]{1,0:T(8,128)(2,1)} async-done(((bf16[1536,768]{1,0:T(8,128)(2,1)}), bf16[1536,768]{1,0:T(8,128)(2,1)}) %all-reduce.14.cloned.1.call-update) | async-done | bytes 2359312 | tf_op jit(solution)/shard_map/psum | solution.py:113
  277.3 4.3 fusion.80
  284.4 4.6 fusion.79
  289.1 7.1 fusion.36
  297.6 7.0 bitcast_convert_fusion.1
  304.7 64.4 %all-gather.9.cloned.1.call-done = bf16[6144,768]{1,0:T(8,128)(2,1)} async-done(((bf16[1536,768]{1,0:T(8,128)(2,1)}), bf16[6144,768]{1,0:T(8,128)(2,1)}) %all-gather.9.cloned.1.call-update) | async-done | bytes 9437200 | tf_op jit(solution)/shard_map/all_gather | solution.py:132
  369.1 6.7 reduce_sum.183
  375.8 6.3 multiply_reduce_fusion.1
  382.2 4.5 fusion.78
  391.4 6.1 fusion.48
  397.5 7.2 multiply_reduce_fusion
  404.7 11.2 %multiply_convert_fusion = bf16[3,3,512,512]{2,3,1,0:T(8,128)(2,1)} fusion(f32[3,3,512,512]{2,3,1,0:T(8,128)} %get-tuple-element.127, f32[3,3,512,512]{2,3,1,0:T(8,128)} %copy-done.2, f32[3,3,512]{2,1,0:T(4,128)S(1)} %get-tuple-element.126, f32[3,3,512]{2,1,0:T(4,128)S(1)} %log_add_fusion), kind=kLoop, calls=%fused_computation.5 | loop fusion | flops 9437184 | bytes 23629824 | tf_op jit(solution)/shard_map/convert_element_type | solution.py:155
  415.9 4.0 fusion.51
  432.4 4.6 fusion.31
  437.1 10.2 %multiply_bitcast_fusion = f32[2,768,768]{1,2,0:T(8,128)} fusion(bf16[1,1536,768]{2,1,0:T(8,128)(2,1)} %get-tuple-element.114, bf16[1,1536,768]{2,1,0:T(8,128)(2,1)} %copy-done.18, f32[1536,768]{1,0:T(8,128)} %copy-done.3, f32[768]{0:T(1024)S(1)} %copy-done.33, f32[768]{0:T(1024)S(1)} %copy-done.26, f32[1536]{0:T(1024)S(1)} %fusion.68, ...), kind=kOutput, calls=%fused_computation.43 | convolution fusion | flops 3633315840 | bytes 14174208 | tf_op jit(solution)/shard_map/td,ktf->kdf/dot_general | solution.py:126
  447.3 8.3 copy.150
  455.7 3.9 convolution_multiply_fusion.3
  462.0 4.3 multiply_bitcast_fusion.1
  466.2 4.2 copy.162
  470.4 4.8 reshape.284
  475.6 6.0 convolution_multiply_fusion
  483.9 5.4 gather_fusion
  489.3 5.4 all-to-all-start.1
  496.0 3.1 convert_reduce_fusion
  499.2 37.9 %all-to-all-done.1 = bf16[8,192,192]{2,1,0:T(8,128)(2,1)S(1)} async-done(((bf16[8,192,192]{2,1,0:T(8,128)(2,1)}), bf16[8,192,192]{2,1,0:T(8,128)(2,1)S(1)}, u32[]{:S(2)}, u32[]{:S(2)}) %all-to-all-start.1) | async-done | bytes 589856 | tf_op jit(solution)/shard_map/all_to_all | solution.py:204
  541.7 5.4 gather_fusion.1
  547.1 3.6 all-to-all-start.3
  550.7 116.5 %all-reduce.16.cloned.1.call-done = f32[2,768,768]{2,0,1:T(2,128)} async-done(((f32[2,768,768]{2,0,1:T(2,128)}), f32[2,768,768]{2,0,1:T(2,128)}) %all-reduce.16.cloned.1.call-update) | async-done | bytes 4718608
  670.7 35.1 %all-reduce.7 = (f32[2,192]{1,0:T(2,128)}, f32[768]{0:T(1024)S(1)}, f32[768]{0:T(1024)S(1)}, f32[768]{0:T(1024)S(1)}, f32[2,768]{1,0:T(2,128)}, /*index=5*/f32[7...) all-reduce(f32[2,192]{1,0:T(2,128)S(1)} %broadcast_multiply_fusion.10, ...), channel_id=1, replica_groups=mesh['dp'=8,'tensor'=4] {'dp'}, use_global_device_ids=true, to_apply=%region_19.20 | all-reduce | flops 6528 | bytes 52224 | tf_op jit(solution)/shard_map/psum | solution.py:199
  709.3 23.4 %reduce-scatter.17.cloned.1.call-done = f32[96,192]{1,0:T(8,128)} async-done(((f32[768,192]{1,0:T(8,128)}), f32[96,192]{1,0:T(8,128)}) %reduce-scatter.17.cloned.1.call-update) | async-done | bytes 73744
  734.3 68.4 %reduce-scatter.15.cloned.1.call-done = f32[96,576]{1,0:T(8,128)} async-done(((f32[768,576]{1,0:T(8,128)}), f32[96,576]{1,0:T(8,128)}) %reduce-scatter.15.cloned.1.call-update) | async-done | bytes 221200
  805.7 69.5 %reduce-scatter.11.cloned.1.call-done = f32[768,96]{0,1:T(8,128)} async-done(((f32[768,768]{0,1:T(8,128)}), f32[768,96]{0,1:T(8,128)}) %reduce-scatter.11.cloned.1.call-update) | async-done | bytes 294928 | tf_op jit(solution)/shard_map/reduce_scatter | solution.py:180
  (226 shorter events, 75.4 us)
Async XLA Ops:
  7.2 190.4 %copy-start = (bf16[2,768,768]{2,1,0:T(8,128)(2,1)S(1)}, bf16[2,768,768]{2,1,0:T(8,128)(2,1)}, u32[]{:S(2)}) copy-start(bf16[2,768,768]{2,1,0:T(8,128)(2,1)} %param.26) | copy-start | bytes 7077892
  7.2 31.4 %copy-start.37 = (s32[1536]{0:T(1024)S(1)}, s32[1536]{0:T(1024)}, u32[]{:S(2)}) copy-start(s32[1536]{0:T(1024)} %param.18) | copy-start | bytes 18436
  7.2 31.5 %copy-start.38 = (s32[1,1536]{1,0:T(1,128)S(1)}, s32[1,1536]{1,0:T(1,128)}, u32[]{:S(2)}) copy-start(s32[1,1536]{1,0:T(1,128)} %param.19) | copy-start | bytes 18436
  7.2 31.5 %copy-start.41 = (bf16[2,192]{1,0:T(2,128)(2,1)S(1)}, bf16[2,192]{1,0:T(2,128)(2,1)}, u32[]{:S(2)}) copy-start(bf16[2,192]{1,0:T(2,128)(2,1)} %param.21) | copy-start | bytes 2308
  7.2 54.5 %all-gather.5.cloned.1.call-start = ((), (), s32[]{:S(2)}) async-start(), calls=%async_computation.8 | async-start | bytes 2949120 | tf_op jit(solution)/shard_map/all_gather | solution.py:67
  38.5 154.5 %all-reduce.12.cloned.1.call-start = ((), (), s32[]{:S(2)}) async-start(), calls=%async_computation.9 | async-start | bytes 9437184 | tf_op jit(solution)/shard_map/psum | solution.py:102
  38.8 184.9 %copy-start.27 = (s32[1536]{0:T(1024)}, s32[1536]{0:T(1024)S(1)}, u32[]{:S(2)}) copy-start(s32[1536]{0:T(1024)S(1)} %fusion.70) | copy-start | bytes 18436
  42.5 33.6 %copy-start.49 = (bf16[3,768,192]{1,2,0:T(8,128)(2,1)S(1)}, bf16[3,768,192]{1,2,0:T(8,128)(2,1)}, u32[]{:S(2)}) copy-start(bf16[3,768,192]{1,2,0:T(8,128)(2,1)} %param.20) | copy-start | bytes 2654212
  98.8 10.2 %copy-start.43 = (bf16[768]{0:T(1024)(128)(2,1)S(1)}, bf16[768]{0:T(1024)(128)(2,1)}, u32[]{:S(2)}) copy-start(bf16[768]{0:T(1024)(128)(2,1)} %param.24) | copy-start | bytes 4612
  98.8 10.3 %copy-start.44 = (bf16[768]{0:T(1024)(128)(2,1)S(1)}, bf16[768]{0:T(1024)(128)(2,1)}, u32[]{:S(2)}) copy-start(bf16[768]{0:T(1024)(128)(2,1)} %param.25) | copy-start | bytes 4612
  98.8 10.3 %copy-start.45 = (bf16[768]{0:T(1024)(128)(2,1)S(1)}, bf16[768]{0:T(1024)(128)(2,1)}, u32[]{:S(2)}) copy-start(bf16[768]{0:T(1024)(128)(2,1)} %param.23) | copy-start | bytes 4612
  98.8 10.3 %copy-start.42 = (bf16[2,768]{1,0:T(2,128)(2,1)S(1)}, bf16[2,768]{1,0:T(2,128)(2,1)}, u32[]{:S(2)}) copy-start(bf16[2,768]{1,0:T(2,128)(2,1)} %param.27) | copy-start | bytes 9220
  103.5 26.2 %all-to-all-start.2 = ((bf16[8,192,192]{1,2,0:T(8,128)(2,1)}), bf16[8,192,192]{1,2,0:T(8,128)(2,1)}, u32[]{:S(2)}, u32[]{:S(2)}) async-start(bf16[8,192,192]{1,2,0:T(8,128)(2,1)} %copy.133), calls=%async_computation.2 | async-start | bytes 1572864 | tf_op jit(solution)/shard_map/all_to_all | solution.py:64
  109.0 110.4 %all-gather.7.cloned.1.call-start = ((), (), s32[]{:S(2)}) async-start(), calls=%async_computation.11 | async-start | bytes 2949120 | tf_op jit(solution)/shard_map/all_gather | solution.py:68
  109.1 168.2 %copy-start.24 = (f32[768]{0:T(1024)}, f32[768]{0:T(1024)S(1)}, u32[]{:S(2)}) copy-start(f32[768]{0:T(1024)S(1)} %convert_element_type.144) | copy-start | bytes 9220
  109.1 168.2 %copy-start.32 = (f32[768]{0:T(1024)}, f32[768]{0:T(1024)S(1)}, u32[]{:S(2)}) copy-start(f32[768]{0:T(1024)S(1)} %convert_element_type.145) | copy-start | bytes 9220
  134.6 142.7 %all-reduce.14.cloned.1.call-start = ((), (), s32[]{:S(2)}) async-start(), calls=%async_computation.10 | async-start | bytes 4718592 | tf_op jit(solution)/shard_map/psum | solution.py:113
  201.8 11.5 %copy-start.8 = (f32[2,1536,768]{2,1,0:T(8,128)}, f32[2,1536,768]{2,1,0:T(8,128)S(1)}, u32[]{:S(2)}) copy-start(f32[2,1536,768]{2,1,0:T(8,128)S(1)} %add_bitcast_fusion) | copy-start | bytes 28311556
  201.8 13.0 %copy-start.48 = (bf16[768,768]{1,0:T(8,128)(2,1)S(1)}, bf16[768,768]{1,0:T(8,128)(2,1)}, u32[]{:S(2)}) copy-start(bf16[768,768]{1,0:T(8,128)(2,1)} %param.28) | copy-start | bytes 3538948
  218.3 150.8 %all-gather.9.cloned.1.call-start = ((), (), s32[]{:S(2)}) async-start(), calls=%async_computation.13 | async-start | bytes 11796480 | tf_op jit(solution)/shard_map/all_gather | solution.py:132
  281.6 7.4 slice-start.2
  281.6 7.4 slice-start.5
  289.0 7.2 copy-start.6
  304.6 233.5 %reduce-scatter.13.cloned.1.call-start = ((), (), s32[]{:S(2)}) async-start(), calls=%async_computation.14 | async-start | bytes 2949120
  369.1 6.7 copy-start.25
  369.1 13.1 %slice-start = ((s8[4718592]{0:T(1024)(128)(4,1)}), s8[524288]{0:T(1024)(128)(4,1)S(1)}, s32[]{:S(2)}) async-start(s8[4718592]{0:T(1024)(128)(4,1)} %bitcast.189), calls=%async_computation.18 | async-start | bytes 1048576
  375.8 6.4 slice-start.1
  404.7 11.2 %copy-start.11 = (bf16[3,512,3,64]{1,0,3,2:T(4,128)(2,1)S(1)}, bf16[3,512,3,64]{1,0,3,2:T(4,128)(2,1)}, u32[]{:S(2)}) copy-start(bf16[3,512,3,64]{1,0,3,2:T(4,128)(2,1)} %copy-done.10) | copy-start | bytes 1769476
  423.0 13.9 %copy-start.12 = (bf16[1,1536,192]{1,2,0:T(8,128)(2,1)}, bf16[1,1536,192]{1,2,0:T(8,128)(2,1)S(1)}, u32[]{:S(2)}) copy-start(bf16[1,1536,192]{1,2,0:T(8,128)(2,1)S(1)} %stack.36) | copy-start | bytes 1769476
  427.7 9.3 %copy-start.13 = (bf16[1,1536,192]{1,2,0:T(8,128)(2,1)}, bf16[1,1536,192]{1,2,0:T(8,128)(2,1)S(1)}, u32[]{:S(2)}) copy-start(bf16[1,1536,192]{1,2,0:T(8,128)(2,1)S(1)} %stack.34) | copy-start | bytes 1769476
  437.0 230.1 %all-reduce.16.cloned.1.call-start = ((), (), s32[]{:S(2)}) async-start(), calls=%async_computation.17 | async-start | bytes 9437184
  455.6 6.3 copy-start.9
  455.6 277.1 %reduce-scatter.17.cloned.1.call-start = ((), (), s32[]{:S(2)}) async-start(), calls=%async_computation.16 | async-start | bytes 884736
  461.9 340.8 %reduce-scatter.15.cloned.1.call-start = ((), (), s32[]{:S(2)}) async-start(), calls=%async_computation.15 | async-start | bytes 2211840
  475.3 6.3 copy-start.40
  475.3 6.4 copy-start.47
  475.3 6.4 copy-start.28
  475.3 399.9 %reduce-scatter.11.cloned.1.call-start = ((), (), s32[]{:S(2)}) async-start(), calls=%async_computation.12 | async-start | bytes 2654208 | tf_op jit(solution)/shard_map/reduce_scatter | solution.py:180
  483.9 10.8 %copy-start.50 = (u32[32]{0:T(128)S(1)}, u32[32]{0:T(128)}, u32[]{:S(2)}) copy-start(u32[32]{0:T(128)} %constant.121) | copy-start | bytes 388
  483.9 12.1 %copy-start.31 = (f32[768]{0:T(1024)S(1)}, f32[768]{0:T(1024)}, u32[]{:S(2)}) copy-start(f32[768]{0:T(1024)} %get-tuple-element.115) | copy-start | bytes 9220
  489.3 47.8 %all-to-all-start.1 = ((bf16[8,192,192]{2,1,0:T(8,128)(2,1)}), bf16[8,192,192]{2,1,0:T(8,128)(2,1)S(1)}, u32[]{:S(2)}, u32[]{:S(2)}) async-start(bf16[8,192,192]{2,1,0:T(8,128)(2,1)} %bitcast.11), calls=%async_computation.1 | async-start | bytes 1572864 | tf_op jit(solution)/shard_map/all_to_all | solution.py:204
  541.7 128.9 %copy-start.29 = (f32[768]{0:T(1024)S(1)}, f32[768]{0:T(1024)}, u32[]{:S(2)}) copy-start(f32[768]{0:T(1024)} %get-tuple-element.101) | copy-start | bytes 9220
  541.7 129.0 %copy-start.30 = (f32[768]{0:T(1024)S(1)}, f32[768]{0:T(1024)}, u32[]{:S(2)}) copy-start(f32[768]{0:T(1024)} %get-tuple-element.90) | copy-start | bytes 9220
  541.7 129.0 %copy-start.36 = (f32[768]{0:T(1024)S(1)}, f32[768]{0:T(1024)}, u32[]{:S(2)}) copy-start(f32[768]{0:T(1024)} %get-tuple-element.84) | copy-start | bytes 9220
  541.7 129.0 %copy-start.34 = (f32[768]{0:T(1024)S(1)}, f32[768]{0:T(1024)}, u32[]{:S(2)}) copy-start(f32[768]{0:T(1024)} %get-tuple-element.86) | copy-start | bytes 9220
  541.7 129.0 %copy-start.35 = (f32[768]{0:T(1024)S(1)}, f32[768]{0:T(1024)}, u32[]{:S(2)}) copy-start(f32[768]{0:T(1024)} %get-tuple-element.87) | copy-start | bytes 9220
  541.7 333.5 %copy-start.1 = (bf16[2,768,768]{2,1,0:T(8,128)(2,1)S(1)}, bf16[2,768,768]{2,1,0:T(8,128)(2,1)}, u32[]{:S(2)}) copy-start(bf16[2,768,768]{2,1,0:T(8,128)(2,1)} %param.26) | copy-start | bytes 7077892
  547.1 257.5 %all-to-all-start.3 = ((bf16[8,192,192]{2,1,0:T(8,128)(2,1)}), bf16[8,192,192]{2,1,0:T(8,128)(2,1)S(1)}, u32[]{:S(2)}, u32[]{:S(2)}) async-start(bf16[8,192,192]{2,1,0:T(8,128)(2,1)} %bitcast.204), calls=%async_computation.3 | async-start | bytes 1572864 | tf_op jit(solution)/shard_map/all_to_all | solution.py:205
  (23 other events, 85.6 us)
Sparse Core Ops, SparseCore 0:
  38.7 23.0 all-gather.4
  99.0 94.0 all-reduce.11
  195.2 24.1 all-gather.6
  221.6 55.6 all-reduce.13
  304.7 64.2 all-gather.8
  437.1 32.8 reduce-scatter.12
  473.6 193.5 all-reduce.15
  670.4 62.2 reduce-scatter.16
  736.2 66.4 reduce-scatter.14
  806.6 68.5 reduce-scatter.10
